TPU v7x, 32 devices: a whole 2x2x4 slice. The times are simulated.
32 devices in a mesh: blk: 8 (over y, x, core), space: 4 (over z).
Axes of the slice: x: 2, y: 2, z: 4, core: 2. Of those that a mesh axis runs over, the one named last changes fastest.
Arguments:
- electrons: bfloat16 [8, 8, 2, 64, 4096], P('blk', None, None, 'space'), may hold values from -4 to 4
- holes: bfloat16 [8, 8, 2, 64, 4096], P('blk', None, None, 'space'), may hold values from -4 to 4
- pair_order: int32 [8, 2], P('blk'), may hold values from 0 to 1, each once within a row
Outputs:
- potential: float32 [8, 2, 64, 64, 128], P('blk', None, 'space')
- coulomb: float32 [8, 2, 2, 2], P('blk')
Inputs may be any that keep to these rules, and one draw needn't show every extreme that they name: `pair_order`: each row lists every candidate once.
All inputs are finite; a program needn't handle non-finite values.
Results may differ from a plain program's by a relative error of at most 0.0003.
Values may be sent and summed in bfloat16 or wider, within the bound.
A program may use at most 64 MiB of HBM per device.

v0:
```python
from functools import partial
import math

import jax
import jax.numpy as jnp
from jax import lax
from jax.sharding import PartitionSpec as P

NX = 64
NY = 64
NZ = 64


SCREENING = 0.01
PRECISE = lax.Precision.HIGHEST


def shifted(block, axis, distance):
    devices = range(lax.axis_size(axis))
    route = [((i - distance) % len(devices), i) for i in devices]
    return lax.ppermute(block, axis, route)


def phase_tables(points, direction):
    positions = jnp.arange(points, dtype=jnp.int32)
    products = positions[:, None] * positions[None, :] % points
    angles = 2.0 * math.pi / points * products.astype(jnp.float32)
    return (jnp.cos(angles), direction * jnp.sin(angles))


def depth_matrix(points, direction):
    cosines, sines = phase_tables(points, direction)
    upper = jnp.concatenate([cosines, -sines], axis=1)
    lower = jnp.concatenate([sines, cosines], axis=1)
    return jnp.concatenate([upper, lower], axis=0)


def turned(values):
    middle = values.shape[-1] // 2
    return jnp.concatenate([values[..., middle:], -values[..., :middle]], axis=-1)


def along_rows(values, direction):
    cosines, sines = phase_tables(values.shape[1], direction)
    tables = jnp.stack([cosines, sines])
    stacked = jnp.stack([values, turned(values)])
    return jnp.einsum("tkn,tpnbc->pkbc", tables, stacked, precision=PRECISE)


def along_columns(values, direction):
    cosines, sines = phase_tables(values.shape[2], direction)
    tables = jnp.stack([cosines, sines])
    stacked = jnp.stack([values, turned(values)])
    return jnp.einsum("tkn,tpanc->pakc", tables, stacked, precision=PRECISE)


def along_depth(values, direction):
    matrix = depth_matrix(values.shape[-1] // 2, direction)
    return jnp.einsum("pabn,nk->pabk", values, matrix, precision=PRECISE)


def lattice_term(indices, points):
    return 2.0 - 2.0 * jnp.cos(2.0 * math.pi / points * (indices % points).astype(jnp.float32))


def green_block(start_y, rows_y):
    index_x = jnp.arange(NX, dtype=jnp.int32)
    index_y = start_y + jnp.arange(rows_y, dtype=jnp.int32)
    index_z = jnp.arange(2 * NZ, dtype=jnp.int32)
    term_x = lattice_term(index_x, NX)
    term_y = lattice_term(index_y, NY)
    term_z = lattice_term(index_z, NZ)
    green = 1.0 / (
        term_x[:, None, None] + term_y[None, :, None] + term_z[None, None, :] + SCREENING
    )
    anchor = (
        (index_x[:, None, None] == 0)
        & (index_y[None, :, None] == 0)
        & (index_z[None, None, :] % NZ == 0)
    )
    return jnp.where(anchor, jnp.zeros_like(green), green)


def pair_densities(electrons, hole_set):

    def banded(first_set, second_set):
        return jnp.einsum(
            "ebxc,hbxc->hexc", first_set, second_set, preferred_element_type=jnp.float32
        )

    real_part = banded(electrons[:, :, 0], hole_set[:, :, 0]) + banded(
        electrons[:, :, 1], hole_set[:, :, 1]
    )
    imag_part = banded(electrons[:, :, 0], hole_set[:, :, 1]) - banded(
        electrons[:, :, 1], hole_set[:, :, 0]
    )
    target_shape = (real_part.shape[0] * real_part.shape[1], real_part.shape[2], NY, NZ)
    return jnp.concatenate(
        [real_part.reshape(target_shape), imag_part.reshape(target_shape)], axis=-1
    )


def fetch_previous(holes):
    return shifted(holes, "blk", 1)


def plane_spectra(densities):
    return along_columns(along_depth(densities, 1.0), 1.0)


def column_spectra(block, start_y):
    spectra = along_rows(block, 1.0)
    return (spectra, spectra * green_block(start_y, block.shape[2])[None])


def finish_inverse(block, factor):
    return along_depth(along_columns(block, -1.0), -1.0) * factor


def inverse_field(weighted, factor):
    return finish_inverse(
        lax.all_to_all(
            along_rows(weighted, -1.0), "space", split_axis=1, concat_axis=2, tiled=True
        ),
        factor=factor,
    )


def pair_products(first_set, second_set):
    flat_first = first_set.reshape(first_set.shape[0], -1)
    stacked = jnp.stack([second_set, -turned(second_set)]).reshape(2, second_set.shape[0], -1)
    return jnp.einsum("pn,tqn->tpq", flat_first, stacked, precision=PRECISE)


def shards(electrons, holes, pair_order):
    rows_y = NY // lax.axis_size("space")
    start_y = lax.axis_index("space") * rows_y
    factor = 1.0 / (NX * NY * NZ)
    forward = partial(column_spectra, start_y=start_y)
    previous = fetch_previous(holes)
    densities = pair_densities(electrons, jnp.concatenate([holes, previous], axis=0))
    spectra, weighted = forward(
        lax.all_to_all(plane_spectra(densities), "space", split_axis=2, concat_axis=1, tiled=True)
    )
    partial_sums = pair_products(weighted, spectra) * (factor * factor)
    potential_field = inverse_field(weighted, factor)
    totals = lax.psum(partial_sums, "space")
    pair_rank = pair_order[0]
    coulomb = jnp.take(jnp.take(totals, pair_rank, axis=1), pair_rank, axis=2)
    potential = jnp.take(potential_field, pair_rank, axis=0)
    return (potential[None], coulomb[None])


def solution(mesh):
    in_specs = (
        P("blk", None, None, "space", None),
        P("blk", None, None, "space", None),
        P("blk", None),
    )
    out_specs = (P("blk", None, "space", None, None), P("blk", None, None, None))
    return jax.shard_map(shards, mesh=mesh, in_specs=in_specs, out_specs=out_specs, check_vma=False)
```

profile of v0, /device:TPU:0, one launch (start us, length us, event | category | flops | bytes accessed | tf_op | source)
XLA Modules:
  0.0 122.4 jit_solution(10038824163050638869)
XLA Ops:
  0.6 0.5 collective-permute-start
  1.3 0.1 fusion.71
  1.4 0.1 fusion.69
  1.6 0.1 fusion.67
  1.7 1.9 %constant_dynamic-update-slice_fusion.1 = bf16[2,8,2,16,4096]{4,3,2,1,0:T(8,128)(2,1)S(1)} fusion(bf16[1,8,2,16,4096]{4,3,2,1,0:T(8,128)(2,1)} %param.4), kind=kLoop, calls=%fused_computation.107 | loop fusion | bytes 4194304
  3.6 0.3 copy-done
  3.9 0.5 bitcast_convert_fusion.1
  4.4 23.6 %collective-permute-done = bf16[1,8,2,16,4096]{4,3,2,1,0:T(8,128)(2,1)S(1)} collective-permute-done((bf16[1,8,2,16,4096]{4,3,2,1,0:T(8,128)(2,1)}, bf16[1,8,2,16,4096]{4,3,2,1,0:T(8,128)(2,1)S(1)}, u32[]{:S(2)}, u32[]{:S(2)}) %collective-permute-start) | collective-permute-done | bytes 2097184 | tf_op jit(solution)/shard_map/ppermute | solution.py:21
  28.0 0.2 constant_dynamic-update-slice_fusion
  28.2 1.7 %fusion.2 = (f32[16,4096,2]{1,0,2:T(8,128)S(1)}, f32[16,4096,2]{1,0,2:T(8,128)S(1)}, f32[16,4096,2]{1,0,2:T(8,128)S(1)}, f32[16,4096,2]{1,0,2:T(8,128)S(1)}) fusion(f32[16,4096,8]{1,0,2:T(8,128)S(1)} %get-tuple-element.9, bf16[2,8,2,16,4096]{4,3,2,1,0:T(8,128)(2,1)S(1)} %constant_dynamic-update-slice_fusion, f32[16,4096,8]{1,0,2:T(8,128)S(1)} %get-tuple-element.8), kind=kLoop, calls=%fused_computation.9 | loop fusion | flops 9961472 | bytes 10485760 | tf_op jit(solution)/shard_map/ebxc,hbxc->hexc/dot_general | solution.py:87
  29.9 0.1 subtract_bitcast_fusion
  30.0 0.4 reshape.326
  30.4 0.4 reshape.325
  30.8 1.1 fusion.32
  31.9 0.4 fusion.95
  32.3 0.3 maximum_bitcast_fusion
  32.7 1.3 %fusion.16 = f32[2,16,64,128]{3,2,0,1:T(8,128)S(1)} fusion(f32[1,64,64]{2,1,0:T(8,128)S(1)} %get-tuple-element.27, f32[1,64,64]{2,1,0:T(8,128)S(1)} %get-tuple-element.26, f32[1,2,16,64,128]{4,3,2,1,0:T(8,128)S(1)} %maximum_bitcast_fusion, f32[1,2,16,64,128]{4,3,2,1,0:T(8,128)S(1)} %bitcast.148), kind=kOutput, calls=%fused_computation.29 | convolution fusion | flops 403185664 | bytes 3178496 | tf_op jit(solution)/shard_map/tkn,tpanc->pakc/dot_general | solution.py:54
  34.0 1.6 %copy.36 = f32[2,16,64,128]{3,1,0,2:T(8,128)} copy(f32[2,16,64,128]{3,2,0,1:T(8,128)S(1)} %fusion.16) | data formatting | bytes 2097152 | tf_op jit(solution)/shard_map/tkn,tpanc->pakc/transpose | solution.py:54
  35.6 5.6 %all-to-all-start = ((f32[2,16,64,128]{3,1,0,2:T(8,128)}), f32[2,16,64,128]{3,1,0,2:T(8,128)S(1)}, u32[]{:S(2)}, u32[]{:S(2)}) async-start(f32[2,16,64,128]{3,1,0,2:T(8,128)} %copy.36), calls=%async_computation | async-start | bytes 2097152 | tf_op jit(solution)/shard_map/all_to_all | solution.py:143
  41.3 0.1 broadcast_multiply_fusion.2
  41.6 1.1 divide_select_fusion
  42.8 22.7 %all-to-all-done = f32[2,16,64,128]{3,1,0,2:T(8,128)S(1)} async-done(((f32[2,16,64,128]{3,1,0,2:T(8,128)}), f32[2,16,64,128]{3,1,0,2:T(8,128)S(1)}, u32[]{:S(2)}, u32[]{:S(2)}) %all-to-all-start) | async-done | bytes 1048608 | tf_op jit(solution)/shard_map/all_to_all | solution.py:143
  65.4 0.1 copy.37
  65.5 0.4 fusion.94
  66.0 0.3 maximum_bitcast_fusion.1
  66.3 0.7 copy-done.1
  67.0 1.3 %broadcast_multiply_fusion = (f32[2,64,16,128]{3,1,2,0:T(8,128)S(1)}, f32[2,16,128,64,1]{2,3,4,1,0:T(8,128)S(1)}) fusion(f32[64,16,128]{2,0,1:T(8,128)S(1)} %copy-done.1, f32[1,64,64]{2,1,0:T(8,128)S(1)} %get-tuple-element.26, f32[1,64,64]{2,1,0:T(8,128)S(1)} %get-tuple-element.27, f32[1,2,64,16,128]{4,2,0,3,1:T(8,128)S(1)} %maximum_bitcast_fusion.1, ...), kind=kOutput, calls=%fused_computation.58 | convolution fusion | flops 403447808 | bytes 4751360 | tf_op jit(solution)/shard_map/tkn,tpnbc->pkbc/dot_general | solution.py:47
  68.3 0.4 fusion.93
  68.7 0.3 maximum_bitcast_fusion.2
  69.1 1.3 %fusion.19 = f32[2,64,16,128]{3,1,0,2:T(8,128)S(1)} fusion(f32[1,64,64]{2,1,0:T(8,128)S(1)} %get-tuple-element.27, f32[1,64,64]{2,1,0:T(8,128)S(1)} %broadcast_multiply_fusion.2, f32[1,2,64,16,128]{4,2,3,1,0:T(8,128)S(1)} %maximum_bitcast_fusion.2, f32[1,2,64,16,128]{4,2,3,1,0:T(8,128)S(1)} %bitcast.151), kind=kOutput, calls=%fused_computation.30 | convolution fusion | flops 403185664 | bytes 3178496 | tf_op jit(solution)/shard_map/tkn,tpnbc->pkbc/dot_general | solution.py:47
  70.4 1.6 %copy.38 = f32[2,64,16,128]{3,2,0,1:T(8,128)} copy(f32[2,64,16,128]{3,1,0,2:T(8,128)S(1)} %fusion.19) | data formatting | bytes 2097152 | tf_op jit(solution)/shard_map/tkn,tpnbc->pkbc/transpose | solution.py:47
  72.0 3.5 %all-to-all-start.1 = ((f32[2,64,16,128]{3,2,0,1:T(8,128)}), f32[2,64,16,128]{3,2,0,1:T(8,128)S(1)}, u32[]{:S(2)}, u32[]{:S(2)}) async-start(f32[2,64,16,128]{3,2,0,1:T(8,128)} %copy.38), calls=%async_computation.1 | async-start | bytes 2097152 | tf_op jit(solution)/shard_map/all_to_all | solution.py:122
  75.5 0.1 broadcast_multiply_fusion.1
  75.7 0.4 slice_bitcast_fusion.2
  76.1 0.3 maximum_negate_fusion
  76.4 0.2 pad_maximum_fusion.3
  76.7 26.4 %fusion.28 = f32[2,2,2]{1,2,0:T(2,128)S(1)} fusion(f32[2,2,64,16,128]{4,2,3,1,0:T(8,128)S(1)} %pad_maximum_fusion.3, f32[2,64,16,128]{3,1,2,0:T(8,128)S(1)} %get-tuple-element.20), kind=kOutput, calls=%fused_computation.34 | convolution fusion | flops 12582920 | bytes 3145760 | tf_op jit(solution)/shard_map/pn,tqn->tpq/dot_general | solution.py:132
  103.1 12.2 %psum.7 = f32[2,2,2]{1,2,0:T(2,128)S(1)} all-reduce(f32[2,2,2]{1,2,0:T(2,128)S(1)} %fusion.28), channel_id=1, replica_groups=mesh['blk'=8,'space'=4] {'space'}, use_global_device_ids=true, to_apply=%region_0.1 | all-reduce | flops 8 | bytes 64 | tf_op jit(solution)/shard_map/psum | solution.py:147
  115.3 0.6 gather_fusion.1
  116.1 0.6 gather_fusion.2
  116.8 0.6 bitcast_select_fusion.1
  117.3 0.1 copy.40
  117.5 0.4 fusion.92
  117.9 0.3 maximum_bitcast_fusion.3
  118.2 1.3 %fusion.8 = f32[2,16,128,64,1]{2,3,0,1,4:T(8,128)S(1)} fusion(f32[1,64,64]{2,1,0:T(8,128)S(1)} %get-tuple-element.27, f32[1,64,64]{2,1,0:T(8,128)S(1)} %broadcast_multiply_fusion.2, f32[1,2,16,64,128]{4,3,2,1,0:T(8,128)S(1)} %maximum_bitcast_fusion.3, f32[1,2,16,64,128]{4,3,2,1,0:T(8,128)S(1)} %bitcast.150), kind=kOutput, calls=%fused_computation.21 | convolution fusion | flops 403185664 | bytes 3178496 | tf_op jit(solution)/shard_map/tkn,tpanc->pakc/dot_general | solution.py:54
  119.5 1.0 convolution_multiply_fusion
  120.6 0.6 gather_fusion
  121.2 1.2 bitcast_select_fusion
  (20 shorter events, 0.7 us)
Async XLA Ops:
  0.6 27.3 %collective-permute-start = (bf16[1,8,2,16,4096]{4,3,2,1,0:T(8,128)(2,1)}, bf16[1,8,2,16,4096]{4,3,2,1,0:T(8,128)(2,1)S(1)}, u32[]{:S(2)}, u32[]{:S(2)}) collective-permute-start(bf16[1,8,2,16,4096]{4,3,2,1,0:T(8,128)(2,1)} %param.4), channel_id=1, source_target_pairs={{28,0},{0,4},{4,8},{8,12},{12,16},{16,20},{20,24},{24,28},{29,1},{... | collective-permute-start | bytes 6291464 | tf_op jit(solution)/shard_map/ppermute | solution.py:21
  1.7 2.2 %copy-start = (bf16[1,8,2,16,4096]{4,3,2,1,0:T(8,128)(2,1)S(1)}, bf16[1,8,2,16,4096]{4,3,2,1,0:T(8,128)(2,1)}, u32[]{:S(2)}) copy-start(bf16[1,8,2,16,4096]{4,3,2,1,0:T(8,128)(2,1)} %param.3) | copy-start | bytes 6291460
  34.0 7.5 %copy-start.2 = (s32[1,2]{1,0:T(1,128)S(1)}, s32[1,2]{1,0:T(1,128)}, u32[]{:S(2)}) copy-start(s32[1,2]{1,0:T(1,128)} %param.5) | copy-start | bytes 28
  35.6 29.8 %all-to-all-start = ((f32[2,16,64,128]{3,1,0,2:T(8,128)}), f32[2,16,64,128]{3,1,0,2:T(8,128)S(1)}, u32[]{:S(2)}, u32[]{:S(2)}) async-start(f32[2,16,64,128]{3,1,0,2:T(8,128)} %copy.36), calls=%async_computation | async-start | bytes 2097152 | tf_op jit(solution)/shard_map/all_to_all | solution.py:143
  66.0 1.0 copy-start.1
  72.0 45.3 %all-to-all-start.1 = ((f32[2,64,16,128]{3,2,0,1:T(8,128)}), f32[2,64,16,128]{3,2,0,1:T(8,128)S(1)}, u32[]{:S(2)}, u32[]{:S(2)}) async-start(f32[2,64,16,128]{3,2,0,1:T(8,128)} %copy.38), calls=%async_computation.1 | async-start | bytes 2097152 | tf_op jit(solution)/shard_map/all_to_all | solution.py:122
where the time goes:
time: 123 us; the launch traced here: 122 us
  waiting for transfers between devices  46.2 us (38%)
  matrix products  33.8 us (27%)
  blocking collectives  12.2 us (10%)
  other arithmetic  10.2 us (8%)
  starting transfers between devices  9.69 us (8%)
  local copies, waits for them, and re-layouts  9.38 us (8%)
    dot_general x1, matrix products, pair_products(): return jnp.einsum('pn,tqn->tpq', flat_first, stacked, precision=PRECISE)  26.4 us
    ppermute x1, waiting for transfers between devices, shifted(): return lax.ppermute(block, axis, route)  23.6 us
    all_to_all x1, waiting for transfers between devices, shards(): lax.all_to_all(plane_spectra(densities), 'space', split_axis=2, concat_ax...  22.7 us
    psum x1, blocking collectives, shards(): totals = lax.psum(partial_sums, 'space')  12.2 us
    all_to_all x1, starting transfers between devices, shards(): lax.all_to_all(plane_spectra(densities), 'space', split_axis=2, concat_ax...  5.62 us
    all_to_all x1, starting transfers between devices, inverse_field(): lax.all_to_all(along_rows(weighted, -1.0), 'space', split_axis=1, concat_...  3.52 us
    unnamed x7, local copies, waits for them, and re-layouts  2.91 us
    dot_general x2, matrix products, along_rows(): return jnp.einsum('tkn,tpnbc->pkbc', tables, stacked, precision=PRECISE)  2.64 us
  transfers between devices with their start and end apart: 3, of which 2 were waited for; matrix products, arithmetic and copies ran while one was open for 28% of the time, Pallas kernels for 0%

commit v1 on v0

v1 whole, which is shorter than its diff:
```python
import functools
import math

import jax
import jax.numpy as jnp
import numpy as np
from jax import lax
from jax.experimental import pallas as pl
from jax.experimental.pallas import tpu as pltpu
from jax.sharding import PartitionSpec as P

SCREENING = 0.01
MESH = pl.DeviceIdType.MESH
LANES = 128
F32 = jnp.float32
BF16 = jnp.bfloat16


def halves(matrix):
    high = matrix.astype(jnp.bfloat16)
    low = (matrix - high.astype(np.float64)).astype(jnp.bfloat16)
    return high, low


def phases(points):
    positions = np.arange(points)
    angles = 2.0 * math.pi / points * (np.outer(positions, positions) % points)
    return np.cos(angles), np.sin(angles)


def depth_table(points, direction):
    cosines, sines = phases(points)
    sines = direction * sines
    matrix = np.concatenate(
        [np.concatenate([cosines, -sines], 1), np.concatenate([sines, cosines], 1)], 0
    )
    high, low = halves(matrix)
    top = np.concatenate([high, low], 1)
    bottom = np.concatenate([high, np.zeros_like(high)], 1)
    return np.concatenate([top, bottom], 0)


def column_table(points, direction):
    cosines, sines = phases(points)
    high, low = halves(np.concatenate([cosines, direction * sines], 1))
    top = np.concatenate([high, high], 1)
    bottom = np.concatenate([low, np.zeros_like(low)], 1)
    return np.concatenate([top, bottom], 0)


def solver_tables(nx, ny, nz, devices):
    term_y = 2.0 - 2.0 * np.cos(2.0 * math.pi / ny * np.arange(ny))
    term_z = 2.0 - 2.0 * np.cos(2.0 * math.pi / nz * (np.arange(2 * nz) % nz))
    shift = term_y[:, None] + term_z[None, :] + SCREENING
    root = np.sqrt(shift * (shift + 4.0))
    decay = 2.0 / (shift + 2.0 + root)
    response = 1.0 / root / (ny * nz)
    anchor = np.zeros_like(shift)
    anchor[0, 0] = anchor[0, nz] = 1.0 / (SCREENING * nx * ny * nz)
    rows = nx // devices
    weights = [decay ** (rows * j) / (1.0 - decay**nx) for j in range(devices)]
    return np.stack([decay, response, anchor] + weights).astype(np.float32)


def split(values):
    high = values.astype(BF16)
    return high, (values - high.astype(F32)).astype(BF16)


def turned(values, sign):
    return pltpu.roll(values, LANES // 2, values.ndim - 1) * sign


def kernel(
    n, blocks, ny,
    order_ref, e_hbm, h_hbm, zf_ref, zi_ref, yf_ref, yi_ref, tab_ref,
    out_ref, coul_ref,
    e_ref, h_ref, prev_ref, acc_ref, rho_ref, fld_ref, res_ref, msg_ref, recv_ref,
    part_ref, peer_ref,
    load_sem, hole_send, hole_recv, msg_send, msg_recv, part_send, part_recv,
):
    bands, _, rows, cells = e_ref.shape
    tiles = cells // LANES
    group = lax.axis_index("blk")
    me = lax.axis_index("space")
    following = lax.rem(group + 1, blocks)
    preceding = lax.rem(group + blocks - 1, blocks)
    others = [lax.rem(me + j, n) for j in range(1, n)]

    loads = [
        pltpu.make_async_copy(e_hbm.at[0], e_ref, load_sem.at[0]),
        pltpu.make_async_copy(h_hbm.at[0], h_ref, load_sem.at[1]),
    ]
    for copy in loads:
        copy.start()

    barrier = pltpu.get_barrier_semaphore()
    for neighbour in (following, preceding):
        pl.semaphore_signal(barrier, inc=1, device_id=(neighbour, me), device_id_type=MESH)
    for other in others:
        pl.semaphore_signal(barrier, inc=1, device_id=(group, other), device_id_type=MESH)
    pl.semaphore_wait(barrier, n + 1)

    hole_copies = [
        pltpu.make_async_remote_copy(
            src_ref=h_hbm.at[0, b], dst_ref=prev_ref.at[b],
            send_sem=hole_send.at[b], recv_sem=hole_recv.at[b],
            device_id=(following, me), device_id_type=MESH,
        )
        for b in range(bands)
    ]
    for copy in hole_copies:
        copy.start()

    lane = lax.broadcasted_iota(jnp.int32, (1, LANES), 1)
    first_half = lane < LANES // 2
    sign = jnp.where(first_half, 1.0, -1.0).astype(F32)

    def products(holes, band_list, t, real, imag):
        window = pl.ds(pl.multiple_of(t * LANES, LANES), LANES)
        for b in band_list:
            er = e_ref[b, 0, :, window].astype(F32)
            ei = e_ref[b, 1, :, window].astype(F32)
            hr = holes[b, 0, :, window].astype(F32)
            hi = holes[b, 1, :, window].astype(F32)
            real = real + (er * hr + ei * hi)
            imag = imag + (er * hi - ei * hr)
        return real, imag

    def place(c, t, real, imag):
        moved_real = pltpu.roll(real, LANES // 2, 1)
        moved_imag = pltpu.roll(imag, LANES // 2, 1)
        rho_ref[c, pl.ds(2 * t, rows, stride=ny), :] = jnp.where(first_half, real, moved_imag)
        rho_ref[c, pl.ds(2 * t + 1, rows, stride=ny), :] = jnp.where(first_half, moved_real, imag)

    planes = min(rows, 4)
    chunk = planes * ny

    def transform(values, z_ref, y_ref):
        high, low = split(values)
        wide = jnp.dot(
            jnp.concatenate([high, low], 1), z_ref[...], preferred_element_type=F32
        )
        deep = wide[:, :LANES] + wide[:, LANES:]
        turn = turned(deep, sign)
        high, low = split(deep)
        turn_high, turn_low = split(turn)
        parts = []
        for x in range(0, planes, 2):
            columns = []
            for k in (x, x + 1):
                own = slice(k * ny, (k + 1) * ny)
                columns.append(
                    jnp.concatenate([high[own], turn_high[own], low[own], turn_low[own]], 0)
                )
            both = jnp.dot(
                y_ref[...], jnp.concatenate(columns, 1), preferred_element_type=F32
            )
            total = both[:ny] + both[ny:]
            parts += [total[:, :LANES], total[:, LANES:]]
        return jnp.concatenate(parts, 0)

    def forward(c):
        @pl.loop(0, rows // planes)
        def _(i):
            own = pl.ds(pl.multiple_of(i * chunk, chunk), chunk)
            rho_ref[c, own, :] = transform(rho_ref[c, own, :], zf_ref, yf_ref)

    block = 16

    def moments(c):
        @pl.loop(0, ny // block)
        def _(i):
            at = pl.multiple_of(i * block, block)
            decay = tab_ref[0, pl.ds(at, block), :]
            left = jnp.zeros((block, LANES), F32)
            right = jnp.zeros((block, LANES), F32)
            for x in range(rows):
                left = decay * left + rho_ref[c, pl.ds(x * ny + at, block), :]
                y = rows - 1 - x
                right = decay * right + rho_ref[c, pl.ds(y * ny + at, block), :]
            msg_ref[c, pl.ds(at, block), :] = left
            msg_ref[c, pl.ds(ny + at, block), :] = right

        total = rho_ref[c, 0:8, :]
        for x in range(1, rows):
            total = total + rho_ref[c, x * ny : x * ny + 8, :]
        msg_ref[c, 2 * ny : 2 * ny + 8, :] = total
        copies = [
            pltpu.make_async_remote_copy(
                src_ref=msg_ref.at[c], dst_ref=recv_ref.at[c, j],
                send_sem=msg_send.at[c, j], recv_sem=msg_recv.at[c, j],
                device_id=(group, others[j]), device_id_type=MESH,
            )
            for j in range(n - 1)
        ]
        for copy in copies:
            copy.start()
        return copies

    def solve(c):
        mean = msg_ref[c, 2 * ny : 2 * ny + 8, :]
        for j in range(n - 1):
            mean = mean + recv_ref[c, j, 2 * ny : 2 * ny + 8, :]
        mean = jnp.concatenate([mean, mean], 0)

        def body(i, energy):
            at = pl.multiple_of(i * block, block)
            decay = tab_ref[0, pl.ds(at, block), :]
            response = tab_ref[1, pl.ds(at, block), :]
            background = tab_ref[2, pl.ds(at, block), :] * mean
            last = tab_ref[2 + n, pl.ds(at, block), :]
            left = last * msg_ref[c, pl.ds(at, block), :]
            right = last * msg_ref[c, pl.ds(ny + at, block), :]
            for j in range(1, n):
                weight = tab_ref[2 + j, pl.ds(at, block), :]
                left = left + weight * recv_ref[c, j - 1, pl.ds(at, block), :]
                right = right + weight * recv_ref[c, n - j - 1, pl.ds(ny + at, block), :]
            spread = []
            for x in reversed(range(rows)):
                right = decay * right
                spread.append(right)
                right = right + rho_ref[c, pl.ds(x * ny + at, block), :]
            for x in range(rows):
                value = rho_ref[c, pl.ds(x * ny + at, block), :]
                left = decay * left + value
                field = response * (left + spread[rows - 1 - x]) - background
                fld_ref[c, pl.ds(x * ny + at, block), :] = field
                energy = energy + field * value
            return energy

        return lax.fori_loop(0, ny // block, body, jnp.zeros((block, LANES), F32))

    for copy in loads:
        copy.wait()

    zero = jnp.zeros((rows, LANES), F32)

    @pl.loop(0, tiles)
    def _(t):
        place(0, t, *products(h_ref, range(bands), t, zero, zero))

    forward(0)
    copies0 = moments(0)

    for b in range(bands):
        hole_copies[b].wait_recv()
        if b == 1:
            for copy in copies0:
                copy.wait_recv()
            part_ref[0:block, :] = solve(0)

            @pl.loop(0, rows // planes)
            def _(i):
                own = pl.ds(pl.multiple_of(i * chunk, chunk), chunk)
                res_ref[own, :] = transform(fld_ref[0, own, :], zi_ref, yi_ref)

        @pl.loop(0, tiles)
        def _(t, b=b):
            window = pl.ds(pl.multiple_of(t * LANES, LANES), LANES)
            if b == 0:
                real, imag = zero, zero
            else:
                real, imag = acc_ref[0, :, window], acc_ref[1, :, window]
            real, imag = products(prev_ref, [b], t, real, imag)
            if b == bands - 1:
                place(1, t, real, imag)
            else:
                acc_ref[0, :, window] = real
                acc_ref[1, :, window] = imag

    forward(1)
    copies1 = moments(1)

    def cross(i, sums):
        at = pl.ds(pl.multiple_of(i * block, block), block)
        field = fld_ref[0, at, :]
        value = rho_ref[1, at, :]
        return sums[0] + field * value, sums[1] - field * turned(value, sign)

    empty = jnp.zeros((block, LANES), F32)
    real, imag = lax.fori_loop(0, rows * ny // block, cross, (empty, empty), unroll=4)
    part_ref[2 * block : 3 * block, :] = real
    part_ref[3 * block : 4 * block, :] = imag

    for copy in copies1:
        copy.wait_recv()
    part_ref[block : 2 * block, :] = solve(1)
    part_copies = [
        pltpu.make_async_remote_copy(
            src_ref=part_ref, dst_ref=peer_ref.at[j],
            send_sem=part_send.at[j], recv_sem=part_recv.at[j],
            device_id=(group, others[j]), device_id_type=MESH,
        )
        for j in range(n - 1)
    ]
    for copy in part_copies:
        copy.start()

    order = [order_ref[0, p] for p in range(2)]

    @pl.loop(0, rows // planes)
    def _(i):
        own = pl.ds(pl.multiple_of(i * chunk, chunk), chunk)
        values = transform(fld_ref[1, own, :], zi_ref, yi_ref)
        stored = res_ref[own, :]
        for p in range(2):
            out_ref[p, own, :] = jnp.where(order[p] == 0, stored, values)

    for copy in part_copies:
        copy.wait_recv()
    entries = []
    for k in range(4):
        own = slice(k * block, (k + 1) * block)
        total = part_ref[own, :]
        for j in range(n - 1):
            total = total + peer_ref[j, own, :]
        entries.append(jnp.sum(total) * (1.0 / (n * rows * cells)))
    for p in range(2):
        for q in range(2):
            same = order[p] == order[q]
            first = order[p] == 0
            coul_ref[2 * p + q] = jnp.where(
                same, jnp.where(first, entries[0], entries[1]), entries[2]
            )
            coul_ref[4 + 2 * p + q] = jnp.where(
                same, 0.0, jnp.where(first, entries[3], -entries[3])
            )

    for copy in hole_copies + copies0 + copies1 + part_copies:
        copy.wait_send()


def shards(n, blocks, electrons, holes, pair_order):
    _, bands, parts, rows, cells = electrons.shape
    ny = nz = math.isqrt(cells)
    flat = rows * ny
    nx = rows * n
    block = 16
    vmem = pl.BlockSpec(memory_space=pltpu.VMEM)
    smem = pl.BlockSpec(memory_space=pltpu.SMEM)
    hbm = pl.BlockSpec(memory_space=pl.ANY)
    states = (bands, parts, rows, cells)
    message = 2 * ny + 8
    potential, coulomb = pl.pallas_call(
        functools.partial(kernel, n, blocks, ny),
        out_shape=(
            jax.ShapeDtypeStruct((2, flat, LANES), F32),
            jax.ShapeDtypeStruct((8,), F32),
        ),
        in_specs=[smem, hbm, hbm, vmem, vmem, vmem, vmem, vmem],
        out_specs=(vmem, smem),
        scratch_shapes=[
            pltpu.VMEM(states, BF16),
            pltpu.VMEM(states, BF16),
            pltpu.VMEM(states, BF16),
            pltpu.VMEM((2, rows, cells), F32),
            pltpu.VMEM((2, flat, LANES), F32),
            pltpu.VMEM((2, flat, LANES), F32),
            pltpu.VMEM((flat, LANES), F32),
            pltpu.VMEM((2, message, LANES), F32),
            pltpu.VMEM((2, n - 1, message, LANES), F32),
            pltpu.VMEM((4 * block, LANES), F32),
            pltpu.VMEM((n - 1, 4 * block, LANES), F32),
            pltpu.SemaphoreType.DMA((2,)),
            pltpu.SemaphoreType.DMA((bands,)),
            pltpu.SemaphoreType.DMA((bands,)),
            pltpu.SemaphoreType.DMA((2, n - 1)),
            pltpu.SemaphoreType.DMA((2, n - 1)),
            pltpu.SemaphoreType.DMA((n - 1,)),
            pltpu.SemaphoreType.DMA((n - 1,)),
        ],
        compiler_params=pltpu.CompilerParams(
            collective_id=0, has_side_effects=True, vmem_limit_bytes=40 * 1024 * 1024
        ),
        name="screened",
    )(
        pair_order,
        electrons,
        holes,
        jnp.asarray(depth_table(nz, 1.0)),
        jnp.asarray(depth_table(nz, -1.0)),
        jnp.asarray(column_table(ny, 1.0)),
        jnp.asarray(column_table(ny, -1.0)),
        jnp.asarray(solver_tables(nx, ny, nz, n)),
    )
    return potential.reshape(1, 2, rows, ny, 2 * nz), coulomb.reshape(1, 2, 2, 2)


def solution(mesh):
    body = functools.partial(shards, mesh.shape["space"], mesh.shape["blk"])
    in_specs = (
        P("blk", None, None, "space", None),
        P("blk", None, None, "space", None),
        P("blk", None),
    )
    out_specs = (P("blk", None, "space", None, None), P("blk", None, None, None))
    return jax.shard_map(body, mesh=mesh, in_specs=in_specs, out_specs=out_specs, check_vma=False)
```

time: 123 us -> 57.7 us (0.47)
  Pallas kernels: 0 us -> 46.8 us
  waiting for transfers between devices: 46.2 us -> 0 us
  matrix products: 33.8 us -> 0 us
  blocking collectives: 12.2 us -> 0 us
  other arithmetic: 10.2 us -> 0 us
  starting transfers between devices: 9.69 us -> 0 us
    pallas_call x0 -> x1, Pallas kernels: none -> 46.8 us  [shards(): pl.pallas_call(functools.partial(kernel, n, blocks, ny), out_shape=(jax.S...]
    dot_general x7 -> x0, matrix products: 33.8 us -> none  [the longest x1 26.4 us: pair_products(): return jnp.einsum('pn,tqn->tpq', flat_first, stacked, precision=PRECISE)]
    ppermute x1 -> x0, waiting for transfers between devices: 23.6 us -> none  [shifted(): return lax.ppermute(block, axis, route)]
    all_to_all x2 -> x0, waiting for transfers between devices: 22.7 us -> none  [the longest x1 22.7 us: shards(): lax.all_to_all(plane_spectra(densities), 'space', split_axis=2, concat_ax...]
    psum x1 -> x0, blocking collectives: 12.2 us -> none  [shards(): totals = lax.psum(partial_sums, 'space')]
    all_to_all x2 -> x0, starting transfers between devices: 9.14 us -> none  [the longest x1 5.62 us: shards(): lax.all_to_all(plane_spectra(densities), 'space', split_axis=2, concat_ax...]
    unnamed x7 -> x17, local copies, waits for them, and re-layouts: 2.91 us -> 9.22 us
    transpose x2 -> x0, local copies, waits for them, and re-layouts: 3.16 us -> none  [the longest x1 1.58 us: along_columns(): return jnp.einsum('tkn,tpanc->pakc', tables, stacked, precision=PRECISE)]
  transfers between devices with their start and end apart: 3 -> 0, of which waited for: 2 -> 0; matrix products, arithmetic and copies ran while one was open for 28% -> 0% of each run, Pallas kernels for 0% -> 0%
where the time goes in v1:
time: 57.7 us; the launch traced here: 57.3 us
  Pallas kernels  46.8 us (81%)
  local copies, waits for them, and re-layouts  9.88 us (17%)
  between operations  0.65 us (1%)
    pallas_call x1, Pallas kernels, shards(): pl.pallas_call(functools.partial(kernel, n, blocks, ny), out_shape=(jax.S...  46.8 us
    unnamed x17, local copies, waits for them, and re-layouts  9.22 us

profile of v1, /device:TPU:0, one launch (start us, length us, event | category | flops | bytes accessed | tf_op | source)
XLA Modules:
  0.0 57.3 jit_solution(13445713085239423000)
XLA Ops:
  0.6 0.0 copy-start
  0.6 1.6 %copy-done = bf16[1,8,2,16,4096]{4,3,2,1,0:T(8,128)(2,1)S(1)} copy-done((bf16[1,8,2,16,4096]{4,3,2,1,0:T(8,128)(2,1)S(1)}, bf16[1,8,2,16,4096]{4,3,2,1,0:T(8,128)(2,1)}, u32[]{:S(2)}) %copy-start) | copy-done | bytes 2097176
  2.2 0.0 copy-start.1
  2.2 1.6 %copy-done.1 = bf16[1,8,2,16,4096]{4,3,2,1,0:T(8,128)(2,1)S(1)} copy-done((bf16[1,8,2,16,4096]{4,3,2,1,0:T(8,128)(2,1)S(1)}, bf16[1,8,2,16,4096]{4,3,2,1,0:T(8,128)(2,1)}, u32[]{:S(2)}) %copy-start.1) | copy-done | bytes 2097176
  3.8 0.0 copy-start.2
  3.8 0.9 %copy-done.2 = f32[7,64,128]{2,1,0:T(8,128)S(1)} copy-done((f32[7,64,128]{2,1,0:T(8,128)S(1)}, f32[7,64,128]{2,1,0:T(8,128)}, u32[]{:S(2)}) %copy-start.2) | copy-done | bytes 229400
  4.8 0.0 copy-start.3
  4.8 0.9 %copy-done.3 = bf16[256,256]{1,0:T(8,128)(2,1)S(1)} copy-done((bf16[256,256]{1,0:T(8,128)(2,1)S(1)}, bf16[256,256]{1,0:T(8,128)(2,1)}, u32[]{:S(2)}) %copy-start.3) | copy-done | bytes 131096
  5.7 0.0 copy-start.4
  5.7 0.9 %copy-done.4 = bf16[256,256]{1,0:T(8,128)(2,1)S(1)} copy-done((bf16[256,256]{1,0:T(8,128)(2,1)S(1)}, bf16[256,256]{1,0:T(8,128)(2,1)}, u32[]{:S(2)}) %copy-start.4) | copy-done | bytes 131096
  6.6 0.0 copy-start.5
  6.6 0.8 %copy-done.5 = bf16[128,256]{1,0:T(8,128)(2,1)S(1)} copy-done((bf16[128,256]{1,0:T(8,128)(2,1)S(1)}, bf16[128,256]{1,0:T(8,128)(2,1)}, u32[]{:S(2)}) %copy-start.5) | copy-done | bytes 65560
  7.4 0.0 copy-start.6
  7.4 0.8 %copy-done.6 = bf16[128,256]{1,0:T(8,128)(2,1)S(1)} copy-done((bf16[128,256]{1,0:T(8,128)(2,1)S(1)}, bf16[128,256]{1,0:T(8,128)(2,1)}, u32[]{:S(2)}) %copy-start.6) | copy-done | bytes 65560
  8.2 0.0 copy-start.7
  8.2 0.7 %copy-done.7 = s32[1,2]{1,0:T(1,128)S(1)} copy-done((s32[1,2]{1,0:T(1,128)S(1)}, s32[1,2]{1,0:T(1,128)}, u32[]{:S(2)}) %copy-start.7) | copy-done | bytes 32
  8.9 46.8 %screened.1 = (f32[2,1024,128]{2,1,0:T(8,128)S(1)}, f32[8]{0:T(128)S(1)}) custom-call(s32[1,2]{1,0:T(1,128)S(1)} %copy-done.7, bf16[1,8,2,16,4096]{4,3,2,1,0:T(8,128)(2,1)S(1)} %copy-done, bf16[1,8,2,16,4096]{4,3,2,1,0:T(8,128)(2,1)S(1)} %copy-done.1, bf16[256,256]{1,0:T(8,128)(2,1)S(1)} %copy-done.4, bf16[256,256]{1,0:T(8,128)(2,1)S(1)} %copy-done.3, ...), custom_call_target="tpu_custom_call" | custom-call | tf_op jit(solution)/shard_map/screened/pallas_call | solution.py:345
  55.7 0.7 %reshape.11 = f32[1,2,2,2]{3,2,1,0:T(2,128)} reshape(f32[8]{0:T(128)S(1)} %get-tuple-element.5) | data formatting | bytes 64 | tf_op jit(solution)/shard_map/reshape | solution.py:387
  56.4 1.0 %copy.11 = f32[1,2,16,64,128]{4,3,2,1,0:T(8,128)} copy(f32[1,2,16,64,128]{4,3,2,1,0:T(8,128)S(1)} %bitcast.1) | data formatting | bytes 2097152
Async XLA Ops:
  0.6 1.6 %copy-start = (bf16[1,8,2,16,4096]{4,3,2,1,0:T(8,128)(2,1)S(1)}, bf16[1,8,2,16,4096]{4,3,2,1,0:T(8,128)(2,1)}, u32[]{:S(2)}) copy-start(bf16[1,8,2,16,4096]{4,3,2,1,0:T(8,128)(2,1)} %e_hbm.1) | copy-start | bytes 6291460
  2.2 1.6 %copy-start.1 = (bf16[1,8,2,16,4096]{4,3,2,1,0:T(8,128)(2,1)S(1)}, bf16[1,8,2,16,4096]{4,3,2,1,0:T(8,128)(2,1)}, u32[]{:S(2)}) copy-start(bf16[1,8,2,16,4096]{4,3,2,1,0:T(8,128)(2,1)} %h_hbm.1) | copy-start | bytes 6291460
  3.8 0.9 %copy-start.2 = (f32[7,64,128]{2,1,0:T(8,128)S(1)}, f32[7,64,128]{2,1,0:T(8,128)}, u32[]{:S(2)}) copy-start(f32[7,64,128]{2,1,0:T(8,128)} %constant.14.clone.tab_ref) | copy-start | bytes 688132
  4.8 0.9 %copy-start.3 = (bf16[256,256]{1,0:T(8,128)(2,1)S(1)}, bf16[256,256]{1,0:T(8,128)(2,1)}, u32[]{:S(2)}) copy-start(bf16[256,256]{1,0:T(8,128)(2,1)} %constant.11.clone.zi_ref) | copy-start | bytes 393220
  5.7 0.9 %copy-start.4 = (bf16[256,256]{1,0:T(8,128)(2,1)S(1)}, bf16[256,256]{1,0:T(8,128)(2,1)}, u32[]{:S(2)}) copy-start(bf16[256,256]{1,0:T(8,128)(2,1)} %constant.10.clone.zf_ref) | copy-start | bytes 393220
  6.6 0.8 %copy-start.5 = (bf16[128,256]{1,0:T(8,128)(2,1)S(1)}, bf16[128,256]{1,0:T(8,128)(2,1)}, u32[]{:S(2)}) copy-start(bf16[128,256]{1,0:T(8,128)(2,1)} %constant.13.clone.yi_ref) | copy-start | bytes 196612
  7.4 0.8 %copy-start.6 = (bf16[128,256]{1,0:T(8,128)(2,1)S(1)}, bf16[128,256]{1,0:T(8,128)(2,1)}, u32[]{:S(2)}) copy-start(bf16[128,256]{1,0:T(8,128)(2,1)} %constant.12.clone.yf_ref) | copy-start | bytes 196612
  8.2 0.7 %copy-start.7 = (s32[1,2]{1,0:T(1,128)S(1)}, s32[1,2]{1,0:T(1,128)}, u32[]{:S(2)}) copy-start(s32[1,2]{1,0:T(1,128)} %order_ref.1) | copy-start | bytes 28

commit v2 on v1

--- a/solution.py
+++ b/solution.py
@@ -73,10 +73,10 @@
 
 def kernel(
     n, blocks, ny,
-    order_ref, e_hbm, h_hbm, zf_ref, zi_ref, yf_ref, yi_ref, tab_ref,
+    order_hbm, e_hbm, h_hbm, phase_hbm, tab_hbm,
     out_ref, coul_ref,
     e_ref, h_ref, prev_ref, acc_ref, rho_ref, fld_ref, res_ref, msg_ref, recv_ref,
-    part_ref, peer_ref,
+    part_ref, peer_ref, order_ref, phase_ref, tab_ref,
     load_sem, hole_send, hole_recv, msg_send, msg_recv, part_send, part_recv,
 ):
     bands, _, rows, cells = e_ref.shape
@@ -90,7 +90,15 @@
     loads = [
         pltpu.make_async_copy(e_hbm.at[0], e_ref, load_sem.at[0]),
         pltpu.make_async_copy(h_hbm.at[0], h_ref, load_sem.at[1]),
+        pltpu.make_async_copy(phase_hbm, phase_ref, load_sem.at[2]),
+        pltpu.make_async_copy(tab_hbm, tab_ref, load_sem.at[3]),
+        pltpu.make_async_copy(order_hbm, order_ref, load_sem.at[4]),
     ]
+    wide = 2 * LANES
+    zf_ref = phase_ref.at[0:wide]
+    zi_ref = phase_ref.at[wide : 2 * wide]
+    yf_ref = phase_ref.at[2 * wide : 2 * wide + LANES]
+    yi_ref = phase_ref.at[2 * wide + LANES : 3 * wide]
     for copy in loads:
         copy.start()
 
@@ -316,16 +324,17 @@
         for j in range(n - 1):
             total = total + peer_ref[j, own, :]
         entries.append(jnp.sum(total) * (1.0 / (n * rows * cells)))
-    for p in range(2):
-        for q in range(2):
-            same = order[p] == order[q]
-            first = order[p] == 0
-            coul_ref[2 * p + q] = jnp.where(
-                same, jnp.where(first, entries[0], entries[1]), entries[2]
-            )
-            coul_ref[4 + 2 * p + q] = jnp.where(
-                same, 0.0, jnp.where(first, entries[3], -entries[3])
-            )
+    shape = (2, 2, 2)
+    part_of = lax.broadcasted_iota(jnp.int32, shape, 0)
+    row = lax.broadcasted_iota(jnp.int32, shape, 1)
+    column = lax.broadcasted_iota(jnp.int32, shape, 2)
+    row_pair = jnp.where(row == 0, order[0], order[1])
+    column_pair = jnp.where(column == 0, order[0], order[1])
+    same = row_pair == column_pair
+    first = row_pair == 0
+    real = jnp.where(same, jnp.where(first, entries[0], entries[1]), entries[2])
+    imag = jnp.where(same, 0.0, jnp.where(first, entries[3], -entries[3]))
+    coul_ref[0] = jnp.where(part_of == 0, real, imag)
 
     for copy in hole_copies + copies0 + copies1 + part_copies:
         copy.wait_send()
@@ -338,18 +347,21 @@
     nx = rows * n
     block = 16
     vmem = pl.BlockSpec(memory_space=pltpu.VMEM)
-    smem = pl.BlockSpec(memory_space=pltpu.SMEM)
     hbm = pl.BlockSpec(memory_space=pl.ANY)
     states = (bands, parts, rows, cells)
     message = 2 * ny + 8
+    phase = np.concatenate(
+        [depth_table(nz, 1.0), depth_table(nz, -1.0), column_table(ny, 1.0), column_table(ny, -1.0)]
+    )
+    tables = solver_tables(nx, ny, nz, n)
     potential, coulomb = pl.pallas_call(
         functools.partial(kernel, n, blocks, ny),
         out_shape=(
             jax.ShapeDtypeStruct((2, flat, LANES), F32),
-            jax.ShapeDtypeStruct((8,), F32),
+            jax.ShapeDtypeStruct((1, 2, 2, 2), F32),
         ),
-        in_specs=[smem, hbm, hbm, vmem, vmem, vmem, vmem, vmem],
-        out_specs=(vmem, smem),
+        in_specs=[hbm] * 5,
+        out_specs=(vmem, vmem),
         scratch_shapes=[
             pltpu.VMEM(states, BF16),
             pltpu.VMEM(states, BF16),
@@ -362,7 +374,10 @@
             pltpu.VMEM((2, n - 1, message, LANES), F32),
             pltpu.VMEM((4 * block, LANES), F32),
             pltpu.VMEM((n - 1, 4 * block, LANES), F32),
-            pltpu.SemaphoreType.DMA((2,)),
+            pltpu.SMEM((1, 2), jnp.int32),
+            pltpu.VMEM(phase.shape, BF16),
+            pltpu.VMEM(tables.shape, F32),
+            pltpu.SemaphoreType.DMA((5,)),
             pltpu.SemaphoreType.DMA((bands,)),
             pltpu.SemaphoreType.DMA((bands,)),
             pltpu.SemaphoreType.DMA((2, n - 1)),
@@ -371,20 +386,17 @@
             pltpu.SemaphoreType.DMA((n - 1,)),
         ],
         compiler_params=pltpu.CompilerParams(
-            collective_id=0, has_side_effects=True, vmem_limit_bytes=40 * 1024 * 1024
+            collective_id=0, has_side_effects=True, vmem_limit_bytes=67_043_328
         ),
         name="screened",
     )(
         pair_order,
         electrons,
         holes,
-        jnp.asarray(depth_table(nz, 1.0)),
-        jnp.asarray(depth_table(nz, -1.0)),
-        jnp.asarray(column_table(ny, 1.0)),
-        jnp.asarray(column_table(ny, -1.0)),
-        jnp.asarray(solver_tables(nx, ny, nz, n)),
+        jnp.asarray(phase),
+        jnp.asarray(tables),
     )
-    return potential.reshape(1, 2, rows, ny, 2 * nz), coulomb.reshape(1, 2, 2, 2)
+    return potential.reshape(1, 2, rows, ny, 2 * nz), coulomb
 
 
 def solution(mesh):

time: 57.7 us -> 50.3 us (0.87)
  local copies, waits for them, and re-layouts: 9.88 us -> 2.89 us
    unnamed x17 -> x4, local copies, waits for them, and re-layouts: 9.22 us -> 2.89 us
    reshape x1 -> x0, local copies, waits for them, and re-layouts: 0.66 us -> none  [shards(): coulomb.reshape(1, 2, 2, 2)]
where the time goes in v2:
time: 50.3 us; the launch traced here: 50.1 us
  Pallas kernels  46.6 us (93%)
  local copies, waits for them, and re-layouts  2.89 us (6%)
  between operations  0.65 us (1%)
    pallas_call x1, Pallas kernels, shards(): pl.pallas_call(functools.partial(kernel, n, blocks, ny), out_shape=(jax.S...  46.6 us
    unnamed x4, local copies, waits for them, and re-layouts  2.89 us

profile of v2, /device:TPU:0, one launch (start us, length us, event | category | flops | bytes accessed | tf_op | source)
XLA Modules:
  0.0 50.1 jit_solution(17021849586525201093)
XLA Ops:
  0.6 46.6 %screened.1 = (f32[2,1024,128]{2,1,0:T(8,128)}, f32[1,2,2,2]{3,2,1,0:T(2,128)}) custom-call(s32[1,2]{1,0:T(1,128)} %order_hbm.1, bf16[1,8,2,16,4096]{4,3,2,1,0:T(8,128)(2,1)} %e_hbm.1, bf16[1,8,2,16,4096]{4,3,2,1,0:T(8,128)(2,1)} %h_hbm.1, bf16[768,256]{1,0:T(8,128)(2,1)} %constant.4.clone.phase_hbm, f32[7,64,128]{2,1,0:T(8,128)} %constant.5.clone.tab_hbm), custom_call_target="tpu_custom_call" | custom-call | tf_op jit(solution)/shard_map/screened/pallas_call | solution.py:357
  47.2 0.0 copy-start
  47.3 2.3 %copy.9 = f32[1,2,16,64,128]{4,3,2,1,0:T(8,128)} copy(f32[1,2,16,64,128]{4,3,2,1,0:T(8,128)} %bitcast.1) | data formatting | bytes 2097152
  49.6 0.0 copy-done
  49.6 0.6 %copy.10 = f32[1,2,2,2]{3,2,1,0:T(2,128)} copy(f32[1,2,2,2]{3,2,1,0:T(2,128)S(1)} %copy-done) | data formatting | bytes 64
Async XLA Ops:
  47.2 2.3 %copy-start = (f32[1,2,2,2]{3,2,1,0:T(2,128)S(1)}, f32[1,2,2,2]{3,2,1,0:T(2,128)}, u32[]{:S(2)}) copy-start(f32[1,2,2,2]{3,2,1,0:T(2,128)} %get-tuple-element.9) | copy-start | bytes 100

commit v3 on v2

--- a/solution.py
+++ b/solution.py
@@ -76,7 +76,7 @@
     order_hbm, e_hbm, h_hbm, phase_hbm, tab_hbm,
     out_ref, coul_ref,
     e_ref, h_ref, prev_ref, acc_ref, rho_ref, fld_ref, res_ref, msg_ref, recv_ref,
-    part_ref, peer_ref, order_ref, phase_ref, tab_ref,
+    part_ref, peer_ref, far_ref, order_ref, phase_ref, tab_ref,
     load_sem, hole_send, hole_recv, msg_send, msg_recv, part_send, part_recv,
 ):
     bands, _, rows, cells = e_ref.shape
@@ -169,7 +169,7 @@
         return jnp.concatenate(parts, 0)
 
     def forward(c):
-        @pl.loop(0, rows // planes)
+        @pl.loop(0, rows // planes, unroll=min(2, rows // planes))
         def _(i):
             own = pl.ds(pl.multiple_of(i * chunk, chunk), chunk)
             rho_ref[c, own, :] = transform(rho_ref[c, own, :], zf_ref, yf_ref)
@@ -206,24 +206,14 @@
             copy.start()
         return copies
 
-    def solve(c):
-        mean = msg_ref[c, 2 * ny : 2 * ny + 8, :]
-        for j in range(n - 1):
-            mean = mean + recv_ref[c, j, 2 * ny : 2 * ny + 8, :]
-        mean = jnp.concatenate([mean, mean], 0)
-
+    empty = jnp.zeros((block, LANES), F32)
+
+    def local(c):
         def body(i, energy):
             at = pl.multiple_of(i * block, block)
             decay = tab_ref[0, pl.ds(at, block), :]
             response = tab_ref[1, pl.ds(at, block), :]
-            background = tab_ref[2, pl.ds(at, block), :] * mean
-            last = tab_ref[2 + n, pl.ds(at, block), :]
-            left = last * msg_ref[c, pl.ds(at, block), :]
-            right = last * msg_ref[c, pl.ds(ny + at, block), :]
-            for j in range(1, n):
-                weight = tab_ref[2 + j, pl.ds(at, block), :]
-                left = left + weight * recv_ref[c, j - 1, pl.ds(at, block), :]
-                right = right + weight * recv_ref[c, n - j - 1, pl.ds(ny + at, block), :]
+            left = right = empty
             spread = []
             for x in reversed(range(rows)):
                 right = decay * right
@@ -232,38 +222,83 @@
             for x in range(rows):
                 value = rho_ref[c, pl.ds(x * ny + at, block), :]
                 left = decay * left + value
-                field = response * (left + spread[rows - 1 - x]) - background
+                field = response * (left + spread[rows - 1 - x])
                 fld_ref[c, pl.ds(x * ny + at, block), :] = field
                 energy = energy + field * value
             return energy
 
-        return lax.fori_loop(0, ny // block, body, jnp.zeros((block, LANES), F32))
+        return lax.fori_loop(0, ny // block, body, empty)
+
+    def solve(c):
+        mean = msg_ref[c, 2 * ny : 2 * ny + 8, :]
+        for k in range(n - 1):
+            mean = mean + recv_ref[c, k, 2 * ny : 2 * ny + 8, :]
+        mean = jnp.concatenate([mean, mean], 0)
+
+        def body(i, energy):
+            at = pl.multiple_of(i * block, block)
+            decay = tab_ref[0, pl.ds(at, block), :]
+            response = tab_ref[1, pl.ds(at, block), :]
+            background = tab_ref[2, pl.ds(at, block), :] * mean
+            weights = [tab_ref[3 + k, pl.ds(at, block), :] for k in range(n)]
+            rights = [msg_ref[c, pl.ds(at, block), :]]
+            lefts = [msg_ref[c, pl.ds(ny + at, block), :]]
+            for k in range(n - 1):
+                rights.append(recv_ref[c, k, pl.ds(at, block), :])
+                lefts.append(recv_ref[c, k, pl.ds(ny + at, block), :])
+            left = right = pairs = empty
+            for a in range(n):
+                coming = empty
+                for k in range(n):
+                    coming = coming + weights[k] * rights[(a + k + 1) % n]
+                pairs = pairs + coming * lefts[a]
+                if a == 0:
+                    left = coming
+            for k in range(n):
+                right = right + weights[k] * lefts[(n - k - 1) % n]
+            energy = energy + 2.0 * response * decay * pairs - background * mean
+            left = response * left
+            right = response * right
+            spread = []
+            for x in range(rows):
+                right = decay * right
+                spread.append(right)
+            for x in range(rows):
+                left = decay * left
+                own = pl.ds(x * ny + at, block)
+                fld_ref[c, own, :] = fld_ref[c, own, :] + (
+                    left + spread[rows - 1 - x] - background
+                )
+            return energy
+
+        return lax.fori_loop(0, ny // block, body, empty)
 
     for copy in loads:
         copy.wait()
 
     zero = jnp.zeros((rows, LANES), F32)
 
-    @pl.loop(0, tiles)
+    @pl.loop(0, tiles, unroll=4)
     def _(t):
         place(0, t, *products(h_ref, range(bands), t, zero, zero))
 
     forward(0)
     copies0 = moments(0)
+    part_ref[0:block, :] = local(0)
 
     for b in range(bands):
         hole_copies[b].wait_recv()
         if b == 1:
             for copy in copies0:
                 copy.wait_recv()
-            part_ref[0:block, :] = solve(0)
-
-            @pl.loop(0, rows // planes)
+            far_ref[0:block, :] = solve(0)
+
+            @pl.loop(0, rows // planes, unroll=min(2, rows // planes))
             def _(i):
                 own = pl.ds(pl.multiple_of(i * chunk, chunk), chunk)
                 res_ref[own, :] = transform(fld_ref[0, own, :], zi_ref, yi_ref)
 
-        @pl.loop(0, tiles)
+        @pl.loop(0, tiles, unroll=4)
         def _(t, b=b):
             window = pl.ds(pl.multiple_of(t * LANES, LANES), LANES)
             if b == 0:
@@ -279,6 +314,7 @@
 
     forward(1)
     copies1 = moments(1)
+    part_ref[block : 2 * block, :] = local(1)
 
     def cross(i, sums):
         at = pl.ds(pl.multiple_of(i * block, block), block)
@@ -286,14 +322,9 @@
         value = rho_ref[1, at, :]
         return sums[0] + field * value, sums[1] - field * turned(value, sign)
 
-    empty = jnp.zeros((block, LANES), F32)
     real, imag = lax.fori_loop(0, rows * ny // block, cross, (empty, empty), unroll=4)
     part_ref[2 * block : 3 * block, :] = real
     part_ref[3 * block : 4 * block, :] = imag
-
-    for copy in copies1:
-        copy.wait_recv()
-    part_ref[block : 2 * block, :] = solve(1)
     part_copies = [
         pltpu.make_async_remote_copy(
             src_ref=part_ref, dst_ref=peer_ref.at[j],
@@ -305,9 +336,13 @@
     for copy in part_copies:
         copy.start()
 
+    for copy in copies1:
+        copy.wait_recv()
+    far_ref[block : 2 * block, :] = solve(1)
+
     order = [order_ref[0, p] for p in range(2)]
 
-    @pl.loop(0, rows // planes)
+    @pl.loop(0, rows // planes, unroll=min(2, rows // planes))
     def _(i):
         own = pl.ds(pl.multiple_of(i * chunk, chunk), chunk)
         values = transform(fld_ref[1, own, :], zi_ref, yi_ref)
@@ -323,6 +358,8 @@
         total = part_ref[own, :]
         for j in range(n - 1):
             total = total + peer_ref[j, own, :]
+        if k < 2:
+            total = total + far_ref[own, :]
         entries.append(jnp.sum(total) * (1.0 / (n * rows * cells)))
     shape = (2, 2, 2)
     part_of = lax.broadcasted_iota(jnp.int32, shape, 0)
@@ -374,6 +411,7 @@
             pltpu.VMEM((2, n - 1, message, LANES), F32),
             pltpu.VMEM((4 * block, LANES), F32),
             pltpu.VMEM((n - 1, 4 * block, LANES), F32),
+            pltpu.VMEM((2 * block, LANES), F32),
             pltpu.SMEM((1, 2), jnp.int32),
             pltpu.VMEM(phase.shape, BF16),
             pltpu.VMEM(tables.shape, F32),

time: 50.3 us -> 44.2 us (0.88)
  Pallas kernels: 46.6 us -> 40.5 us
    pallas_call x1, Pallas kernels: 46.6 us -> 40.5 us  [shards(): pl.pallas_call(functools.partial(kernel, n, blocks, ny), out_shape=(jax.S...]
where the time goes in v3:
time: 44.2 us; the launch traced here: 44.1 us
  Pallas kernels  40.5 us (92%)
  local copies, waits for them, and re-layouts  2.89 us (7%)
  between operations  0.65 us (1%)
    pallas_call x1, Pallas kernels, shards(): pl.pallas_call(functools.partial(kernel, n, blocks, ny), out_shape=(jax.S...  40.5 us
    unnamed x4, local copies, waits for them, and re-layouts  2.89 us

profile of v3, /device:TPU:0, one launch (start us, length us, event | category | flops | bytes accessed | tf_op | source)
XLA Modules:
  0.0 44.1 jit_solution(10174187319429294972)
XLA Ops:
  0.6 40.5 %screened.1 = (f32[2,1024,128]{2,1,0:T(8,128)}, f32[1,2,2,2]{3,2,1,0:T(2,128)}) custom-call(s32[1,2]{1,0:T(1,128)} %order_hbm.1, bf16[1,8,2,16,4096]{4,3,2,1,0:T(8,128)(2,1)} %e_hbm.1, bf16[1,8,2,16,4096]{4,3,2,1,0:T(8,128)(2,1)} %h_hbm.1, bf16[768,256]{1,0:T(8,128)(2,1)} %constant.4.clone.phase_hbm, f32[7,64,128]{2,1,0:T(8,128)} %constant.5.clone.tab_hbm), custom_call_target="tpu_custom_call" | custom-call | tf_op jit(solution)/shard_map/screened/pallas_call | solution.py:394
  41.2 0.0 copy-start
  41.2 2.3 %copy.9 = f32[1,2,16,64,128]{4,3,2,1,0:T(8,128)} copy(f32[1,2,16,64,128]{4,3,2,1,0:T(8,128)} %bitcast.1) | data formatting | bytes 2097152
  43.5 0.0 copy-done
  43.5 0.6 %copy.10 = f32[1,2,2,2]{3,2,1,0:T(2,128)} copy(f32[1,2,2,2]{3,2,1,0:T(2,128)S(1)} %copy-done) | data formatting | bytes 64
Async XLA Ops:
  41.2 2.3 %copy-start = (f32[1,2,2,2]{3,2,1,0:T(2,128)S(1)}, f32[1,2,2,2]{3,2,1,0:T(2,128)}, u32[]{:S(2)}) copy-start(f32[1,2,2,2]{3,2,1,0:T(2,128)} %get-tuple-element.9) | copy-start | bytes 100
